TPU v7x, 256 devices: a whole 4x4x8 slice. The times are simulated.
256 devices in a mesh: dp: 32 (over x, z), tensor: 8 (over y, core).
Axes of the slice: x: 4, y: 4, z: 8, core: 2. Of those that a mesh axis runs over, the one named last changes fastest.
Arguments:
- activations: bfloat16 [2048, 24, 14336], P('dp', None, 'tensor'), may hold values from -6 to 6
- out_grads: bfloat16 [2048, 24, 4096], P('dp', None, 'tensor'), may hold values from -6 to 6
- proj_in: bfloat16 [14336, 64], P('tensor'), may hold values from -0.046875 to 0.046875
- proj_out: bfloat16 [4096, 64], P('tensor'), may hold values from -0.09375 to 0.09375
- queries: bfloat16 [32, 5120, 4096], P('dp', 'tensor'), may hold values from -0.09375 to 0.09375
- candidates: int32 [2048, 4], P('dp'), may hold values from 0 to 31, all different within a row; in each aligned block of 64 rows (0 to 63, 64 to 127, ...) at most 20 rows name the same one
Outputs:
- scores: float32 [2048, 4, 5120], P('dp', None, 'tensor')
Inputs may be any that keep to these rules, and one draw needn't show every extreme that they name: `candidates`: each example names 4 different groups. Among the 64 examples of one index of dp at most 20 name the same group, and in every draw some group is named by exactly 20 of them.
All inputs are finite; a program needn't handle non-finite values.
Results may differ from a plain program's by a relative error of at most 0.0029.
Values may be sent and summed in bfloat16 or wider, within the bound.
A program may use at most 64 MiB of HBM per device.

v0:
```python
import jax
import jax.numpy as jnp
from jax import lax
from jax.sharding import PartitionSpec as P

epsilon = 1e-06


def local(activations, out_grads, proj_in, proj_out, queries, candidates):
    examples_here, tokens_here, hidden_here = activations.shape
    proj_rank = proj_in.shape[1]
    per_example = candidates.shape[1]
    groups = lax.axis_size("dp")
    capacity = max(2, 5 * examples_here * per_example // (2 * groups))
    act_proj = jnp.dot(
        activations.reshape(examples_here * tokens_here, hidden_here),
        proj_in,
        preferred_element_type=jnp.float32,
    )
    grad_proj = jnp.dot(
        out_grads.reshape(examples_here * tokens_here, out_grads.shape[2]),
        proj_out,
        preferred_element_type=jnp.float32,
    )
    both_proj = jnp.concatenate([grad_proj, act_proj], axis=1).reshape(
        examples_here, tokens_here, 2 * proj_rank
    )
    summed = lax.psum(both_proj, "tensor")
    grad_side = summed[:, :, :proj_rank]
    act_side = summed[:, :, proj_rank:]
    example_grads = jnp.einsum(
        "eta,etb->eab", grad_side, act_side, precision=lax.Precision.HIGHEST
    ).reshape(examples_here, proj_rank * proj_rank)
    inv_rms = lax.rsqrt(jnp.mean(example_grads * example_grads, axis=1, keepdims=True) + epsilon)
    unit_grads = (example_grads * inv_rms).astype(jnp.bfloat16)
    flat_cands = candidates.reshape(-1)
    hit_table = (flat_cands[:, None] == jnp.arange(groups, dtype=jnp.int32)[None, :]).astype(
        jnp.int32
    )
    earlier = jnp.cumsum(hit_table, axis=0) - hit_table
    slot_index = jnp.sum(earlier * hit_table, axis=1)
    dest_index = flat_cands * capacity + slot_index
    row_copies = jnp.repeat(unit_grads, per_example, axis=0)
    grad_width = unit_grads.shape[1]
    send_buffer = (
        jnp.zeros((groups * capacity, grad_width), jnp.bfloat16).at[dest_index].set(row_copies)
    )
    send_buffer = send_buffer.reshape(groups, capacity, grad_width)
    query_block = queries[0]
    slot_scores = jnp.einsum(
        "gsk,qk->gsq",
        lax.all_to_all(send_buffer, "dp", split_axis=0, concat_axis=0, tiled=True),
        query_block,
        preferred_element_type=jnp.float32,
    )
    returned = lax.all_to_all(slot_scores, "dp", split_axis=0, concat_axis=0, tiled=True)
    picked = returned.reshape(groups * capacity, returned.shape[2])[dest_index]
    return picked.reshape(examples_here, per_example, returned.shape[2])


def solution(mesh):
    placed = (
        P("dp", None, "tensor"),
        P("dp", None, "tensor"),
        P("tensor", None),
        P("tensor", None),
        P("dp", "tensor", None),
        P("dp", None),
    )
    return jax.shard_map(
        local, mesh=mesh, in_specs=placed, out_specs=P("dp", None, "tensor"), check_vma=False
    )
```

profile of v0, /device:TPU:24, one launch (start us, length us, event | category | flops | bytes accessed | tf_op | source)
XLA Modules:
  0.0 337.4 jit_solution(5751738510498375177)
XLA Ops:
  6.5 0.0 all-reduce.2.cloned.1.call-start
  6.5 1.4 copy-done
  7.9 1.4 fusion.11
  9.4 0.0 copy-start.1
  9.4 4.3 %fusion.12 = f32[1536,64]{0,1:T(8,128)S(1)} fusion(bf16[1536,1792]{1,0:T(8,128)(2,1)} %bitcast.34, bf16[1792,64]{0,1:T(8,128)(2,1)} %param.8), kind=kOutput, calls=%fused_computation.26 | convolution fusion | flops 352321536 | bytes 6127616 | tf_op jit(solution)/shard_map/dot_general | solution.py:15
  13.7 0.1 pad_maximum_fusion
  13.8 1.1 copy.19
  14.9 0.0 all-reduce.2.cloned.1.call-update
  15.0 0.1 copy.16
  15.1 0.1 eq.29
  15.2 0.6 reduce-window.6
  15.8 0.2 slice_reduce_fusion
  16.0 0.1 eq.25
  16.1 0.1 copy.15
  16.2 0.1 mul.33
  16.3 0.1 fusion.9
  16.4 66.1 %all-reduce.2.cloned.1.call-done = f32[64,24,128]{2,1,0:T(8,128)} async-done(((f32[64,24,128]{2,1,0:T(8,128)}), f32[64,24,128]{2,1,0:T(8,128)}) %all-reduce.2.cloned.1.call-update) | async-done | bytes 786448 | tf_op jit(solution)/shard_map/psum | solution.py:28
  82.6 7.0 %multiply_reduce_fusion = (f32[64]{0:T(128)S(1)}, f32[64,64,64]{2,1,0:T(8,128)}) fusion(f32[64,24,128]{2,1,0:T(8,128)} %all-reduce.2.cloned.1.call-done), kind=kOutput, calls=%fused_computation.6 | convolution fusion | flops 76021696 | bytes 2621696 | tf_op jit(solution)/shard_map/eta,etb->eab/dot_general | solution.py:31
  89.5 2.1 reshape.82
  91.7 0.1 multiply_convert_fusion
  91.8 2.3 broadcast_in_dim.5
  94.1 4.0 %reshape.99 = bf16[256,4096]{1,0:T(8,128)(2,1)} reshape(bf16[64,4,4096]{2,1,0:T(4,128)(2,1)} %broadcast_in_dim.5) | data formatting | bytes 4194304 | tf_op jit(solution)/shard_map/reshape | solution.py:43
  98.1 7.7 %scatter_custom_fusion = bf16[640,4096]{1,0:T(8,128)(2,1)} fusion(s32[256]{0:T(256)S(1)} %bitcast.36, bf16[256,4096]{1,0:T(8,128)(2,1)} %reshape.99, bf16[]{:T(256)} %constant.7.clone.1), kind=kCustom, calls=%fused_computation.4 | custom fusion | bytes 5243392 | tf_op jit(solution)/shard_map/scatter | solution.py:46
  105.8 7.8 %reshape.84 = bf16[32,20,4096]{2,1,0:T(8,128)(2,1)} reshape(bf16[640,4096]{1,0:T(8,128)(2,1)} %scatter_custom_fusion) | data formatting | bytes 10485760 | tf_op jit(solution)/shard_map/reshape | solution.py:48
  113.6 151.8 %all_to_all.10 = bf16[32,20,4096]{2,1,0:T(8,128)(2,1)S(1)} all-to-all(bf16[32,20,4096]{2,1,0:T(8,128)(2,1)} %reshape.84), channel_id=1, replica_groups=mesh['dp'=32,'tensor'=8] {'dp'}, dimensions={0} | all-to-all | bytes 10485760 | tf_op jit(solution)/shard_map/all_to_all | solution.py:52
  265.4 0.0 slice-done
  265.4 6.5 %fusion = f32[32,20,640]{2,1,0:T(8,128)} fusion(bf16[32,20,4096]{2,1,0:T(8,128)(2,1)S(1)} %all_to_all.10, bf16[1,640,4096]{2,1,0:T(8,128)(2,1)S(1)} %bitcast.40), kind=kOutput, calls=%fused_computation.2 | convolution fusion | flops 3355443200 | bytes 12124160 | tf_op jit(solution)/shard_map/gsk,qk->gsq/dot_general | solution.py:50
  271.9 5.5 %all-to-all-start.1 = ((f32[32,20,640]{2,1,0:T(8,128)}), f32[32,20,640]{2,1,0:T(8,128)}, u32[]{:S(2)}, u32[]{:S(2)}) async-start(f32[32,20,640]{2,1,0:T(8,128)} %fusion), calls=%async_computation.1 | async-start | bytes 3932160 | tf_op jit(solution)/shard_map/all_to_all | solution.py:56
  277.4 47.6 %all-to-all-done.1 = f32[32,20,640]{2,1,0:T(8,128)} async-done(((f32[32,20,640]{2,1,0:T(8,128)}), f32[32,20,640]{2,1,0:T(8,128)}, u32[]{:S(2)}, u32[]{:S(2)}) %all-to-all-start.1) | async-done | bytes 1638432 | tf_op jit(solution)/shard_map/all_to_all | solution.py:56
  325.0 1.6 reshape.85
  326.6 1.9 gather_fusion
  328.5 2.1 reshape.86
  (13 shorter events, 0.1 us)
Async XLA Ops:
  6.5 1.4 copy-start
  6.5 76.0 %all-reduce.2.cloned.1.call-start = ((), (), s32[]{:S(2)}) async-start(), calls=%async_computation.2 | async-start | bytes 1572864 | tf_op jit(solution)/shard_map/psum | solution.py:28
  9.4 5.6 %copy-start.1 = (s32[64,4]{0,1:T(4,128)S(1)}, s32[64,4]{0,1:T(4,128)}, u32[]{:S(2)}) copy-start(s32[64,4]{0,1:T(4,128)} %param.11) | copy-start | bytes 3076
  105.8 159.6 %slice-start = ((s8[5242880]{0:T(1024)(128)(4,1)}), s8[1048576]{0:T(1024)(128)(4,1)S(1)}, s32[]{:S(2)}) async-start(s8[5242880]{0:T(1024)(128)(4,1)} %bitcast.39), calls=%async_computation.3 | async-start | bytes 2097152
  113.6 151.8 %slice-start.1 = ((s8[5242880]{0:T(1024)(128)(4,1)}), s8[4194304]{0:T(1024)(128)(4,1)S(1)}, s32[]{:S(2)}) async-start(s8[5242880]{0:T(1024)(128)(4,1)} %bitcast.39), calls=%async_computation.4 | async-start | bytes 8388608
  271.9 53.1 %all-to-all-start.1 = ((f32[32,20,640]{2,1,0:T(8,128)}), f32[32,20,640]{2,1,0:T(8,128)}, u32[]{:S(2)}, u32[]{:S(2)}) async-start(f32[32,20,640]{2,1,0:T(8,128)} %fusion), calls=%async_computation.1 | async-start | bytes 3932160 | tf_op jit(solution)/shard_map/all_to_all | solution.py:56
Sparse Core Ops, SparseCore 0:
  15.1 67.4 all-reduce.1
where the time goes:
time: 338 us; the launch traced here: 337 us
  blocking collectives  152 us (45%)
  waiting for transfers between devices  114 us (34%)
  local copies, waits for them, and re-layouts  32.8 us (10%)
  matrix products  19.2 us (6%)
  between operations  13.5 us (4%)
  starting transfers between devices  5.54 us (2%)
    all_to_all x1, blocking collectives, local(): lax.all_to_all(send_buffer, 'dp', split_axis=0, concat_axis=0, tiled=True)  152 us
    psum x1, waiting for transfers between devices, local(): summed = lax.psum(both_proj, 'tensor')  66.1 us
    all_to_all x1, waiting for transfers between devices, local(): lax.all_to_all(slot_scores, 'dp', split_axis=0, concat_axis=0, tiled=True)  47.6 us
    reshape x1, local copies, waits for them, and re-layouts, local(): send_buffer = send_buffer.reshape(groups, capacity, grad_width)  7.78 us
    scatter x1, local copies, waits for them, and re-layouts, local(): jnp.zeros((groups * capacity, grad_width), jnp.bfloat16).at[dest_index]  7.75 us
    dot_general x1, matrix products, local(): jnp.einsum('eta,etb->eab', grad_side, act_side, precision=lax.Precision.H...  6.96 us
  transfers between devices with their start and end apart: 2, of which 2 were waited for; matrix products, arithmetic and copies ran while one was open for 0% of the time, Pallas kernels for 0%

commit v1 on v0

--- a/solution.py
+++ b/solution.py
@@ -25,7 +25,7 @@
     both_proj = jnp.concatenate([grad_proj, act_proj], axis=1).reshape(
         examples_here, tokens_here, 2 * proj_rank
     )
-    summed = lax.psum(both_proj, "tensor")
+    summed = jnp.sum(lax.all_gather(both_proj, "tensor"), axis=0)
     grad_side = summed[:, :, :proj_rank]
     act_side = summed[:, :, proj_rank:]
     example_grads = jnp.einsum(

time: 338 us -> 317 us (0.938)
  waiting for transfers between devices: 114 us -> 89.9 us
    psum x1 -> x0, waiting for transfers between devices: 66.1 us -> none  [local(): summed = lax.psum(both_proj, 'tensor')]
    all_gather x0 -> x1, waiting for transfers between devices: none -> 42.9 us  [local(): summed = jnp.sum(lax.all_gather(both_proj, 'tensor'), axis=0)]
where the time goes in v1:
time: 317 us; the launch traced here: 315 us
  blocking collectives  151 us (48%)
  waiting for transfers between devices  89.9 us (28%)
  local copies, waits for them, and re-layouts  32.8 us (10%)
  matrix products  17.8 us (6%)
  between operations  13.5 us (4%)
  starting transfers between devices  5.22 us (2%)
  other arithmetic  4.11 us (1%)
    all_to_all x1, blocking collectives, local(): lax.all_to_all(send_buffer, 'dp', split_axis=0, concat_axis=0, tiled=True)  151 us
    all_to_all x1, waiting for transfers between devices, local(): lax.all_to_all(slot_scores, 'dp', split_axis=0, concat_axis=0, tiled=True)  47 us
    all_gather x1, waiting for transfers between devices, local(): summed = jnp.sum(lax.all_gather(both_proj, 'tensor'), axis=0)  42.9 us
    reshape x1, local copies, waits for them, and re-layouts, local(): send_buffer = send_buffer.reshape(groups, capacity, grad_width)  7.78 us
    scatter x1, local copies, waits for them, and re-layouts, local(): jnp.zeros((groups * capacity, grad_width), jnp.bfloat16).at[dest_index]  7.75 us
    dot_general x1, matrix products, local(): jnp.einsum('gsk,qk->gsq', lax.all_to_all(send_buffer, 'dp', split_axis=0,...  6.46 us
  transfers between devices with their start and end apart: 2, of which 2 were waited for; matrix products, arithmetic and copies ran while one was open for 0% of the time, Pallas kernels for 0%

profile of v1, /device:TPU:24, one launch (start us, length us, event | category | flops | bytes accessed | tf_op | source)
XLA Modules:
  0.0 314.8 jit_solution(15812162282688348709)
XLA Ops:
  6.5 0.0 all-gather.2.cloned.1.call-start
  6.5 1.4 copy-done
  7.9 1.4 fusion.11
  9.4 0.0 copy-start.1
  9.4 4.3 %fusion.12 = f32[1536,64]{0,1:T(8,128)S(1)} fusion(bf16[1536,1792]{1,0:T(8,128)(2,1)} %bitcast.34, bf16[1792,64]{0,1:T(8,128)(2,1)} %param.8), kind=kOutput, calls=%fused_computation.26 | convolution fusion | flops 352321536 | bytes 6127616 | tf_op jit(solution)/shard_map/dot_general | solution.py:15
  13.7 0.1 pad_maximum_fusion
  13.8 1.2 copy.18
  14.9 0.0 all-gather.2.cloned.1.call-update
  15.0 0.1 copy.15
  15.1 0.1 eq.29
  15.2 0.1 eq.25
  15.3 0.6 reduce-window.6
  15.9 0.2 slice_reduce_fusion
  16.1 0.1 copy.14
  16.2 0.1 mul.33
  16.3 0.1 fusion.9
  16.4 42.9 %all-gather.2.cloned.1.call-done = f32[8,64,24,128]{3,2,1,0:T(8,128)} async-done(((f32[1,64,24,128]{3,2,1,0:T(8,128)}), f32[8,64,24,128]{3,2,1,0:T(8,128)}) %all-gather.2.cloned.1.call-update) | async-done | bytes 6291472 | tf_op jit(solution)/shard_map/all_gather | solution.py:28
  59.3 3.2 %reduce_sum.31 = f32[64,24,128]{2,1,0:T(8,128)S(1)} reduce(f32[8,64,24,128]{3,2,1,0:T(8,128)} %all-gather.2.cloned.1.call-done, f32[]{:T(128)} %constant.6.clone.1), dimensions={0}, to_apply=%region_3.4 | reduce | flops 1376256 | bytes 7077892 | tf_op jit(solution)/shard_map/reduce_sum | solution.py:28
  62.5 5.6 %multiply_reduce_fusion = (f32[64]{0:T(128)S(1)}, f32[64,64,64]{2,1,0:T(8,128)}) fusion(f32[64,24,128]{2,1,0:T(8,128)S(1)} %reduce_sum.31), kind=kOutput, calls=%fused_computation.6 | convolution fusion | flops 76021696 | bytes 2621696 | tf_op jit(solution)/shard_map/eta,etb->eab/dot_general | solution.py:31
  68.1 2.1 reshape.78
  70.2 0.1 multiply_convert_fusion
  70.4 2.3 broadcast_in_dim.5
  72.7 4.0 %reshape.95 = bf16[256,4096]{1,0:T(8,128)(2,1)} reshape(bf16[64,4,4096]{2,1,0:T(4,128)(2,1)} %broadcast_in_dim.5) | data formatting | bytes 4194304 | tf_op jit(solution)/shard_map/reshape | solution.py:43
  76.7 7.7 %scatter_custom_fusion = bf16[640,4096]{1,0:T(8,128)(2,1)} fusion(s32[256]{0:T(256)S(1)} %bitcast.36, bf16[256,4096]{1,0:T(8,128)(2,1)} %reshape.95, bf16[]{:T(256)} %constant.7.clone.1), kind=kCustom, calls=%fused_computation.4 | custom fusion | bytes 5243392 | tf_op jit(solution)/shard_map/scatter | solution.py:46
  84.4 7.8 %reshape.80 = bf16[32,20,4096]{2,1,0:T(8,128)(2,1)} reshape(bf16[640,4096]{1,0:T(8,128)(2,1)} %scatter_custom_fusion) | data formatting | bytes 10485760 | tf_op jit(solution)/shard_map/reshape | solution.py:48
  92.2 151.4 %all_to_all.10 = bf16[32,20,4096]{2,1,0:T(8,128)(2,1)S(1)} all-to-all(bf16[32,20,4096]{2,1,0:T(8,128)(2,1)} %reshape.80), channel_id=1, replica_groups=mesh['dp'=32,'tensor'=8] {'dp'}, dimensions={0} | all-to-all | bytes 10485760 | tf_op jit(solution)/shard_map/all_to_all | solution.py:52
  243.6 6.5 %fusion = f32[32,20,640]{2,1,0:T(8,128)} fusion(bf16[32,20,4096]{2,1,0:T(8,128)(2,1)S(1)} %all_to_all.10, bf16[1,640,4096]{2,1,0:T(8,128)(2,1)S(1)} %bitcast.40), kind=kOutput, calls=%fused_computation.2 | convolution fusion | flops 3355443200 | bytes 12124160 | tf_op jit(solution)/shard_map/gsk,qk->gsq/dot_general | solution.py:50
  250.1 5.2 %all-to-all-start.1 = ((f32[32,20,640]{2,1,0:T(8,128)}), f32[32,20,640]{2,1,0:T(8,128)}, u32[]{:S(2)}, u32[]{:S(2)}) async-start(f32[32,20,640]{2,1,0:T(8,128)} %fusion), calls=%async_computation.1 | async-start | bytes 3932160 | tf_op jit(solution)/shard_map/all_to_all | solution.py:56
  255.3 47.0 %all-to-all-done.1 = f32[32,20,640]{2,1,0:T(8,128)} async-done(((f32[32,20,640]{2,1,0:T(8,128)}), f32[32,20,640]{2,1,0:T(8,128)}, u32[]{:S(2)}, u32[]{:S(2)}) %all-to-all-start.1) | async-done | bytes 1638432 | tf_op jit(solution)/shard_map/all_to_all | solution.py:56
  302.3 1.6 reshape.81
  303.9 1.9 gather_fusion
  305.8 2.1 reshape.82
  (14 shorter events, 0.1 us)
Async XLA Ops:
  6.5 1.4 copy-start
  6.5 52.8 %all-gather.2.cloned.1.call-start = ((), (), s32[]{:S(2)}) async-start(), calls=%async_computation.2 | async-start | bytes 7077888 | tf_op jit(solution)/shard_map/all_gather | solution.py:28
  9.4 5.6 %copy-start.1 = (s32[64,4]{0,1:T(4,128)S(1)}, s32[64,4]{0,1:T(4,128)}, u32[]{:S(2)}) copy-start(s32[64,4]{0,1:T(4,128)} %param.11) | copy-start | bytes 3076
  84.4 159.2 %slice-start = ((s8[5242880]{0:T(1024)(128)(4,1)}), s8[1048576]{0:T(1024)(128)(4,1)S(1)}, s32[]{:S(2)}) async-start(s8[5242880]{0:T(1024)(128)(4,1)} %bitcast.39), calls=%async_computation.3 | async-start | bytes 2097152
  92.2 151.5 %slice-start.1 = ((s8[5242880]{0:T(1024)(128)(4,1)}), s8[4194304]{0:T(1024)(128)(4,1)S(1)}, s32[]{:S(2)}) async-start(s8[5242880]{0:T(1024)(128)(4,1)} %bitcast.39), calls=%async_computation.4 | async-start | bytes 8388608
  250.1 52.2 %all-to-all-start.1 = ((f32[32,20,640]{2,1,0:T(8,128)}), f32[32,20,640]{2,1,0:T(8,128)}, u32[]{:S(2)}, u32[]{:S(2)}) async-start(f32[32,20,640]{2,1,0:T(8,128)} %fusion), calls=%async_computation.1 | async-start | bytes 3932160 | tf_op jit(solution)/shard_map/all_to_all | solution.py:56
Sparse Core Ops, SparseCore 0:
  15.1 44.1 all-gather.1
